TPU v7x, 32 devices: a whole 2x2x4 slice. The times are simulated.
32 devices in a mesh: scheme: 8 (over z, y), scen: 4 (over x, core).
Axes of the slice: x: 2, y: 2, z: 4, core: 2. Of those that a mesh axis runs over, the one named last changes fastest.
Arguments:
- cashflow: bfloat16 [1024, 400], P('scheme'), may hold values from 0.00049972534 to 0.0099487305
- assets0: float32 [1024], P('scheme'), may hold values from 0.5 to 2
- alloc: int32 [1024, 3], P('scheme'), may hold values from 0 to 39
- share: float32 [1024, 3], P('scheme'), may hold values from 0.2 to 1
- owner: int32 [1024, 1], P('scheme'), may hold values from 0 to 7; in each aligned block of 128 rows (0 to 127, 128 to 255, ...) at most 32 rows name the same one
- flags: int32 [1024, 2, 1024], P('scheme', None, 'scen'), may hold values 0 or 1
- rates: float32 [2, 100, 1024], P(None, None, 'scen'), may hold values from 0.0035 to 0.07
- inflation: float32 [2, 100, 1024], P(None, None, 'scen'), may hold values from 0 to 0.056
- returns: float32 [2, 40, 1024], P(None, None, 'scen'), may hold values from -0.6 to 0.6
- basis: bfloat16 [8, 400, 1024], P('scheme', None, 'scen'), may hold values from 0.37 to 1.96
Outputs:
- book: float32 [8, 2, 1024], P('scheme', None, 'scen')
- levy: float32 [1024, 2, 1024], P('scheme', None, 'scen')
Inputs may be any that keep to these rules, and one draw needn't show every extreme that they name: Among the 128 schemes of one device's aligned block, no book owner is named more than 32 times, a bound that some block reaches.
All inputs are finite; a program needn't handle non-finite values. No bound on the sum of `flags` on one device may be relied on, other than what follows from the above.
Results may differ from a plain program's by a relative error of at most 0.0005.
Values may be sent and summed in bfloat16 or wider, within the bound.
A program may use at most 64 MiB of HBM per device.

v0:
```python
import jax
import jax.numpy as jnp
from jax import lax
from jax.sharding import PartitionSpec as P

TRANCHE_INDEX = (0.0, 0.5, 1.0, 0.75)
COMP_LIMIT = 0.004


def discount(rate_year, infl_year):
    horizon = rate_year.shape[0]
    terms = (jnp.arange(horizon) + 1).astype(jnp.float32)[None, :, None]
    index = jnp.asarray(TRANCHE_INDEX, jnp.float32)[:, None, None]
    power = -terms * (rate_year[None] - index * infl_year[None])
    return jnp.exp(power).reshape(4 * horizon, rate_year.shape[1]).astype(jnp.bfloat16)


def shards(cashflow, assets0, alloc, share, owner, flags, rates, inflation, returns, basis):
    scheme_rows = cashflow.shape[0]
    width = cashflow.shape[1]
    years = rates.shape[0]
    scen_local = rates.shape[2]
    classes = returns.shape[1]
    groups = lax.axis_size("scheme")
    slot_cap = max(2, (2 * scheme_rows + groups - 1) // groups)
    picks = (alloc[:, :, None] == jnp.arange(classes, dtype=jnp.int32)[None, None, :]).astype(
        jnp.float32
    )
    exposure = jnp.sum(picks * share[:, :, None], axis=1)
    comp = jnp.minimum(0.9 * cashflow.astype(jnp.float32), COMP_LIMIT).astype(jnp.bfloat16)
    assets = jnp.broadcast_to(assets0[:, None], (scheme_rows, scen_local))
    base_part = jnp.zeros((scheme_rows,), jnp.float32)
    factor_list = []
    held = []
    for year in range(years):
        disc = discount(rates[year], inflation[year])
        liab = jnp.dot(cashflow, disc, preferred_element_type=jnp.float32)
        growth = jnp.dot(exposure, returns[year], precision=lax.Precision.HIGHEST)
        assets = assets * jnp.exp(growth)
        base_part = base_part + jnp.sum(jnp.maximum(liab - assets, 0.0) + 0.05 * liab, axis=1)
        factor_list.append(
            (basis[0].astype(jnp.float32) * disc.astype(jnp.float32)).astype(jnp.bfloat16)
        )
        held.append(assets)
    held_all = jnp.stack(held, axis=1)
    scen_total = scen_local * lax.axis_size("scen")
    base = lax.psum(base_part, "scen") / (scen_total * years)
    owners_of = owner[:, 0]
    hits = (owners_of[:, None] == jnp.arange(groups, dtype=jnp.int32)[None, :]).astype(jnp.int32)
    earlier = jnp.cumsum(hits, axis=0) - hits
    rank = jnp.sum(earlier * hits, axis=1)
    slot_pos = owners_of * slot_cap + rank
    send_rows = jnp.zeros((groups * slot_cap, width), jnp.bfloat16).at[slot_pos].set(comp)
    send_rows = send_rows.reshape(groups, slot_cap, width)
    flag_vals = flags.astype(jnp.float32)
    selector = hits.astype(jnp.float32)
    rows = lax.all_to_all(send_rows, "scheme", split_axis=0, concat_axis=0, tiled=True)
    count = rows.shape[1]
    value_count = rows.shape[1]
    flat = rows.reshape(groups * value_count, width)
    values = [
        jnp.dot(flat, factor_list[year], preferred_element_type=jnp.float32)
        for year in range(years)
    ]
    values = jnp.stack(values, axis=1).reshape(groups, count, years * scen_local)
    back = lax.all_to_all(values, "scheme", split_axis=0, concat_axis=0, tiled=True)
    mine = back.reshape(groups * slot_cap, years, scen_local)[slot_pos]
    net = flag_vals * (mine - held_all)
    term = net.reshape(scheme_rows, years * scen_local)
    book_share = lax.psum_scatter(
        jnp.dot(selector.T, term, precision=lax.Precision.HIGHEST),
        "scheme",
        scatter_dimension=0,
        tiled=True,
    )
    book = book_share.reshape(1, years, scen_local)
    claim_input = book[0]
    claims, base_total = lax.psum((claim_input, jnp.sum(base)), "scheme")
    levy = (claims / groups)[None] * base[:, None, None] / (base_total / (scheme_rows * groups))
    return (book, levy)


def solution(mesh):
    placed = (
        P("scheme", None),
        P("scheme"),
        P("scheme", None),
        P("scheme", None),
        P("scheme", None),
        P("scheme", None, "scen"),
        P(None, None, "scen"),
        P(None, None, "scen"),
        P(None, None, "scen"),
        P("scheme", None, "scen"),
    )
    return jax.shard_map(
        shards,
        mesh=mesh,
        in_specs=placed,
        out_specs=(P("scheme", None, "scen"), P("scheme", None, "scen")),
        check_vma=False,
    )
```

profile of v0, /device:TPU:0, one launch (start us, length us, event | category | flops | bytes accessed | tf_op | source)
XLA Modules:
  0.0 100.3 jit_solution(16488516456864838028)
XLA Ops:
  0.6 0.6 copy-done.7
  1.7 0.5 copy-done.1
  2.4 1.7 %scatter_custom_fusion = bf16[256,400]{1,0:T(8,128)(2,1)} fusion(s32[128]{0:T(128)S(1)} %fusion.28, bf16[128,400]{1,0:T(8,128)(2,1)S(1)} %copy.46, bf16[]{:T(256)} %constant.13.clone.1), kind=kCustom, calls=%fused_computation.36 | custom fusion | bytes 204802 | tf_op jit(solution)/shard_map/scatter | solution.py:53
  4.2 7.4 %all-to-all-start = ((bf16[8,32,400]{2,1,0:T(8,128)(2,1)}), bf16[8,32,400]{2,1,0:T(8,128)(2,1)S(1)}, u32[]{:S(2)}, u32[]{:S(2)}) async-start(bf16[8,32,400]{2,1,0:T(8,128)(2,1)} %bitcast.3), calls=%async_computation | async-start | bytes 524288 | tf_op jit(solution)/shard_map/all_to_all | solution.py:57
  11.8 0.8 copy-done.5
  12.8 0.6 copy-done.11
  13.9 0.8 sub.63
  14.7 5.8 %all-to-all-done = bf16[8,32,400]{2,1,0:T(8,128)(2,1)S(1)} async-done(((bf16[8,32,400]{2,1,0:T(8,128)(2,1)}), bf16[8,32,400]{2,1,0:T(8,128)(2,1)S(1)}, u32[]{:S(2)}, u32[]{:S(2)}) %all-to-all-start) | async-done | bytes 204832 | tf_op jit(solution)/shard_map/all_to_all | solution.py:57
  20.9 0.6 copy-done
  22.4 1.2 %reshape.227 = f32[8,32,512]{2,1,0:T(8,128)} reshape(f32[256,2,256]{2,1,0:T(2,128)S(1)} %copy.51) | data formatting | bytes 1048576 | tf_op jit(solution)/shard_map/reshape | solution.py:65
  23.6 3.7 %all-to-all-start.1 = ((f32[8,32,512]{2,1,0:T(8,128)}), f32[8,32,512]{2,1,0:T(8,128)S(1)}, u32[]{:S(2)}, u32[]{:S(2)}) async-start(f32[8,32,512]{2,1,0:T(8,128)} %reshape.227), calls=%async_computation.1 | async-start | bytes 1048576 | tf_op jit(solution)/shard_map/all_to_all | solution.py:66
  27.9 0.6 copy-done.12
  28.5 0.6 dynamic-slice
  29.9 0.5 add_reduce_fusion
  30.3 6.2 %psum.22 = f32[128]{0:T(128)S(1)} all-reduce(f32[128]{0:T(128)S(1)} %add.45), channel_id=1, replica_groups=mesh['scheme'=8,'scen'=4] {'scen'}, use_global_device_ids=true, to_apply=%region_8.9 | all-reduce | flops 128 | bytes 1024 | tf_op jit(solution)/shard_map/psum | solution.py:47
  36.6 0.7 broadcast_multiply_fusion.1
  37.3 4.2 %all-to-all-done.1 = f32[8,32,512]{2,1,0:T(8,128)S(1)} async-done(((f32[8,32,512]{2,1,0:T(8,128)}), f32[8,32,512]{2,1,0:T(8,128)S(1)}, u32[]{:S(2)}, u32[]{:S(2)}) %all-to-all-start.1) | async-done | bytes 524320 | tf_op jit(solution)/shard_map/all_to_all | solution.py:66
  41.8 0.9 gather_fusion
  43.4 35.2 %all-reduce = f32[8,512]{1,0:T(8,128)S(1)} all-reduce(f32[8,512]{1,0:T(8,128)S(1)} %fusion.19), channel_id=2, replica_groups=mesh['scheme'=8,'scen'=4] {'scheme'}, use_global_device_ids=true, to_apply=%region_4.0.clone | all-reduce | flops 4096 | bytes 32768
  78.6 0.5 broadcast.134
  79.1 1.3 %fusion.30 = (f32[512]{0:T(512)S(1)}, f32[1,512]{1,0:T(1,128)S(1)}) fusion(f32[]{:T(128)} %broadcast.134, f32[8,512]{1,0:T(8,128)S(1)} %all-reduce, u32[]{:T(128)} %bitcast.20), kind=kLoop, calls=%fused_computation.63 | loop fusion | bytes 6152
  80.4 0.6 reshape.230
  81.0 17.7 %all-reduce.1 = (f32[]{:T(128)}, f32[2,256]{1,0:T(2,128)S(1)}) all-reduce(f32[]{:T(128)} %get-tuple-element.11, f32[2,256]{1,0:T(2,128)S(1)} %squeeze_reshape.3), channel_id=1, replica_groups=mesh['scheme'=8,'scen'=4] {'scheme'}, use_global_device_ids=true, to_apply=%region_10.11 | all-reduce | flops 513 | bytes 4104 | tf_op jit(solution)/shard_map/psum | solution.py:78
  99.4 0.9 multiply_divide_fusion
  (62 shorter events, 5.0 us)
Async XLA Ops:
  0.6 0.7 copy-start.7
  1.4 0.9 copy-start.1
  4.2 7.4 %copy-start.4 = (f32[2,100,256]{2,0,1:T(2,128)S(1)}, f32[2,100,256]{2,0,1:T(2,128)}, u32[]{:S(2)}) copy-start(f32[2,100,256]{2,0,1:T(2,128)} %param.18) | copy-start | bytes 614404
  4.2 16.3 %all-to-all-start = ((bf16[8,32,400]{2,1,0:T(8,128)(2,1)}), bf16[8,32,400]{2,1,0:T(8,128)(2,1)S(1)}, u32[]{:S(2)}, u32[]{:S(2)}) async-start(bf16[8,32,400]{2,1,0:T(8,128)(2,1)} %bitcast.3), calls=%async_computation | async-start | bytes 524288 | tf_op jit(solution)/shard_map/all_to_all | solution.py:57
  11.6 0.9 copy-start.5
  12.7 0.7 copy-start.11
  13.9 0.8 copy-start.8
  13.9 0.8 copy-start.9
  13.9 6.6 %copy-start.2 = (bf16[1,400,256]{2,1,0:T(8,128)(2,1)S(1)}, bf16[1,400,256]{2,1,0:T(8,128)(2,1)}, u32[]{:S(2)}) copy-start(bf16[1,400,256]{2,1,0:T(8,128)(2,1)} %param.21) | copy-start | bytes 614404
  20.5 1.0 copy-start
  23.6 3.7 %copy-start.6 = (f32[2,40,256]{2,1,0:T(8,128)S(1)}, f32[2,40,256]{2,1,0:T(8,128)}, u32[]{:S(2)}) copy-start(f32[2,40,256]{2,1,0:T(8,128)} %param.20) | copy-start | bytes 245764
  23.6 3.7 %copy-start.10 = (f32[128]{0:T(128)S(1)}, f32[128]{0:T(128)}, u32[]{:S(2)}) copy-start(f32[128]{0:T(128)} %param.13) | copy-start | bytes 1540
  23.6 17.9 %all-to-all-start.1 = ((f32[8,32,512]{2,1,0:T(8,128)}), f32[8,32,512]{2,1,0:T(8,128)S(1)}, u32[]{:S(2)}, u32[]{:S(2)}) async-start(f32[8,32,512]{2,1,0:T(8,128)} %reshape.227), calls=%async_computation.1 | async-start | bytes 1048576 | tf_op jit(solution)/shard_map/all_to_all | solution.py:66
  27.8 0.7 copy-start.12
  41.8 1.0 copy-start.3
where the time goes:
time: 101 us; the launch traced here: 100 us
  blocking collectives  59.2 us (59%)
  local copies, waits for them, and re-layouts  13.5 us (13%)
  starting transfers between devices  11.1 us (11%)
  waiting for transfers between devices  10 us (10%)
  matrix products  2.72 us (3%)
  other arithmetic  2.17 us (2%)
  between operations  1.63 us (2%)
    unnamed x1, blocking collectives  35.2 us
    psum x1, blocking collectives, shards(): claims, base_total = lax.psum((claim_input, jnp.sum(base)), 'scheme')  17.7 us
    all_to_all x1, starting transfers between devices, shards(): lax.all_to_all(send_rows, 'scheme', split_axis=0, concat_axis=0, tiled=True)  7.41 us
    unnamed x29, local copies, waits for them, and re-layouts  6.26 us
    psum x1, blocking collectives, shards(): base = lax.psum(base_part, 'scen') / (scen_total * years)  6.24 us
    all_to_all x1, waiting for transfers between devices, shards(): lax.all_to_all(send_rows, 'scheme', split_axis=0, concat_axis=0, tiled=True)  5.8 us
    all_to_all x1, waiting for transfers between devices, shards(): lax.all_to_all(values, 'scheme', split_axis=0, concat_axis=0, tiled=True)  4.21 us
    all_to_all x1, starting transfers between devices, shards(): lax.all_to_all(values, 'scheme', split_axis=0, concat_axis=0, tiled=True)  3.72 us
  transfers between devices with their start and end apart: 2, of which 2 were waited for; matrix products, arithmetic and copies ran while one was open for 5% of the time, Pallas kernels for 0%

commit v1 on v0

v1 whole, which is shorter than its diff:
```python
import functools

import jax
import jax.numpy as jnp
from jax import lax
from jax.experimental import pallas as pl
from jax.experimental.pallas import tpu as pltpu
from jax.sharding import PartitionSpec as P

TRANCHE_INDEX = (0.0, 0.5, 1.0, 0.75)
COMP_LIMIT = 0.004
HIGHEST = lax.Precision.HIGHEST
NT = (((1,), (1,)), ((), ()))
TN = (((0,), (0,)), ((), ()))


def each(low, high, body):
    if high - low <= 16:
        for i in range(low, high):
            body(i)
    else:
        lax.fori_loop(low, high, lambda i, c: (body(i), c)[1], 0)


def block(i, size):
    start = i * size
    return pl.ds(start if isinstance(start, int) else pl.multiple_of(start, size), size)


def kernel(groups, pad, parts,
           owner_h, cash_h, flags_h, rates_h, infl_h, returns_h, alloc_h, share_h, assets0_h, basis_h,
           book_ref, coef_ref, base_ref,
           owner_v, cash_v, flags_v, rates_v, infl_v, returns_v, alloc_v, share_v, assets0_v, basis_v,
           comp_send, comp_recv, flag_send, flag_recv, disc_v, held_send, held_recv,
           base_send, base_recv, claim_send, claim_recv,
           local_sem, comp_ss, comp_rs, flag_ss, flag_rs, held_ss, held_rs, base_ss, base_rs, claim_ss, claim_rs):
    g = lax.axis_index("scheme")
    c = lax.axis_index("scen")
    rows = owner_v.shape[1]
    years = rates_v.shape[1]
    hor = rates_v.shape[0]
    n = rates_v.shape[2]
    classes = returns_v.shape[1]

    def local(k, src, dst):
        copy = pltpu.make_async_copy(src, dst, local_sem.at[k])
        copy.start()
        return copy

    in_owner = local(0, owner_h, owner_v)
    in_flags = local(1, flags_h, flags_v)
    in_cash = local(2, cash_h, cash_v)
    in_rates = local(3, rates_h, rates_v)
    in_infl = local(4, infl_h, infl_v)
    in_returns = local(5, returns_h, returns_v)
    in_alloc = local(6, alloc_h, alloc_v)
    in_share = local(7, share_h, share_v)
    in_assets0 = local(8, assets0_h, assets0_v)
    in_basis = local(9, basis_h, basis_v)

    barrier = pltpu.get_barrier_semaphore()

    def greet(i):
        pl.semaphore_signal(barrier, inc=1, device_id={"scheme": lax.rem(g + i, groups)})

    def greet_scen(i):
        pl.semaphore_signal(barrier, inc=1, device_id={"scen": lax.rem(c + i, parts)})

    each(1, groups, greet)
    each(1, parts, greet_scen)

    def to_scheme(src, dst, ss, rs, i):
        return pltpu.make_async_remote_copy(
            src_ref=src, dst_ref=dst, send_sem=ss.at[i], recv_sem=rs.at[i],
            device_id={"scheme": lax.rem(g + i, groups)})

    def comp_copy(i):
        return to_scheme(comp_send.at[block(i, pad)], comp_recv.at[block(i, pad)], comp_ss, comp_rs, i)

    def flag_copy(i):
        return to_scheme(flag_send.at[block(i, pad)], flag_recv.at[block(i, pad)], flag_ss, flag_rs, i)

    def held_copy(i):
        return to_scheme(held_send.at[i], held_recv.at[i], held_ss, held_rs, i)

    def claim_copy(i):
        return to_scheme(claim_send, claim_recv.at[i], claim_ss, claim_rs, i)

    def base_copy(i):
        return pltpu.make_async_remote_copy(
            src_ref=base_send, dst_ref=base_recv.at[i], send_sem=base_ss.at[i], recv_sem=base_rs.at[i],
            device_id={"scen": lax.rem(c + i, parts)})

    in_owner.wait()
    rel = lax.rem(owner_v[...] - g + groups, groups)
    hits = (rel == lax.broadcasted_iota(jnp.int32, (groups, rows), 0)).astype(jnp.float32)
    upper = (lax.broadcasted_iota(jnp.int32, (rows, rows), 0)
             < lax.broadcasted_iota(jnp.int32, (rows, rows), 1)).astype(jnp.bfloat16)
    earlier = jnp.dot(hits.astype(jnp.bfloat16), upper, preferred_element_type=jnp.float32)
    rank = jnp.sum(earlier * hits, axis=0, keepdims=True).astype(jnp.int32)
    slot = rel * pad + rank
    pick = (slot == lax.broadcasted_iota(jnp.int32, (groups * pad, rows), 0)).astype(jnp.bfloat16)

    in_flags.wait()
    flags = [flags_v[:, y, :].astype(jnp.float32) for y in range(years)]
    for y in range(years):
        flag_send[:, y * n:(y + 1) * n] = jnp.dot(
            pick, flags[y].astype(jnp.bfloat16), preferred_element_type=jnp.float32).astype(jnp.bfloat16)
    in_cash.wait()
    cash_t = cash_v[...]
    comp_t = jnp.minimum(0.9 * cash_t.astype(jnp.float32), COMP_LIMIT).astype(jnp.bfloat16)
    comp_send[...] = lax.dot_general(
        pick, comp_t, NT, preferred_element_type=jnp.float32).astype(jnp.bfloat16)

    pl.semaphore_wait(barrier, groups + parts - 2)
    each(1, groups, lambda i: comp_copy(i).start())
    each(1, groups, lambda i: flag_copy(i).start())
    comp_recv[0:pad] = comp_send[0:pad]
    flag_recv[0:pad] = flag_send[0:pad]

    in_returns.wait()
    in_alloc.wait()
    in_share.wait()
    in_assets0.wait()
    eye = (lax.broadcasted_iota(jnp.int32, (rows, rows), 0)
           == lax.broadcasted_iota(jnp.int32, (rows, rows), 1))
    class_id = lax.broadcasted_iota(jnp.int32, (classes, rows), 0)
    exposure_t = jnp.zeros((classes, rows), jnp.float32)
    for j in range(alloc_v.shape[0]):
        exposure_t = exposure_t + jnp.where(alloc_v[j:j + 1, :] == class_id, share_v[j:j + 1, :], 0.0)
    assets = jnp.sum(jnp.where(eye, assets0_v[...], 0.0), axis=1, keepdims=True)
    held = []
    for y in range(years):
        growth = lax.dot_general(exposure_t, returns_v[y], TN, precision=HIGHEST,
                                 preferred_element_type=jnp.float32)
        assets = assets * jnp.exp(growth)
        held.append(assets)
        held_send[:, y, :] = jnp.dot(hits, flags[y] * assets, precision=HIGHEST,
                                     preferred_element_type=jnp.float32)
    each(1, groups, lambda i: held_copy(i).start())

    in_rates.wait()
    in_infl.wait()
    neg_terms = -(lax.broadcasted_iota(jnp.int32, (hor, n), 0) + 1).astype(jnp.float32)
    short = jnp.zeros((rows, n), jnp.float32)
    for y in range(years):
        rate = rates_v[:, y, :]
        infl = infl_v[:, y, :]
        for k, index in enumerate(TRANCHE_INDEX):
            disc_v[y, k * hor:(k + 1) * hor, :] = jnp.exp(neg_terms * (rate - index * infl))
        liab = lax.dot_general(cash_t, disc_v[y].astype(jnp.bfloat16), TN,
                               preferred_element_type=jnp.float32)
        short = short + (jnp.maximum(liab - held[y], 0.0) + 0.05 * liab)
    base_send[...] = lax.dot_general(jnp.ones((8, n), jnp.float32), short, NT, precision=HIGHEST,
                                     preferred_element_type=jnp.float32)
    each(1, parts, lambda i: base_copy(i).start())

    in_basis.wait()
    basis = basis_v[0].astype(jnp.float32)
    factors = [(basis * disc_v[y].astype(jnp.bfloat16).astype(jnp.float32)).astype(jnp.bfloat16)
               for y in range(years)]
    each(1, groups, lambda i: comp_copy(i).wait_recv())
    each(1, groups, lambda i: flag_copy(i).wait_recv())
    book = []
    for y in range(years):
        value = jnp.dot(comp_recv[...], factors[y], preferred_element_type=jnp.float32)
        weight = flag_recv[:, y * n:(y + 1) * n].astype(jnp.float32)
        book.append(jnp.sum(weight * value, axis=0, keepdims=True))
    each(1, groups, lambda i: held_copy(i).wait_recv())
    held_recv[0] = held_send[0]
    for y in range(years):
        book[y] = book[y] - jnp.sum(held_recv[:, y, :], axis=0, keepdims=True)
        claim_send[y:y + 1, :] = book[y]
        book_ref[0, y:y + 1, :] = book[y]

    each(1, parts, lambda i: base_copy(i).wait_recv())
    base = base_send[0:1, :]
    for i in range(1, parts):
        base = base + base_recv[i, 0:1, :]
    base = base / (n * parts * years)
    base_ref[...] = base
    claim_send[years:years + 1, :] = jnp.broadcast_to(jnp.sum(base, axis=1, keepdims=True), (1, n))
    each(1, groups, lambda i: claim_copy(i).start())
    claim_recv[0] = claim_send[...]
    each(1, groups, lambda i: claim_copy(i).wait_recv())
    total = jnp.sum(claim_recv[...], axis=0)
    for y in range(years):
        coef_ref[y:y + 1, :] = (total[y:y + 1, :] / groups) / (total[years:years + 1, :] / (rows * groups))

    each(1, groups, lambda i: comp_copy(i).wait_send())
    each(1, groups, lambda i: flag_copy(i).wait_send())
    each(1, groups, lambda i: held_copy(i).wait_send())
    each(1, parts, lambda i: base_copy(i).wait_send())
    each(1, groups, lambda i: claim_copy(i).wait_send())


def shards(cashflow, assets0, alloc, share, owner, flags, rates, inflation, returns, basis):
    rows, width = cashflow.shape
    years, hor, n = rates.shape
    classes = returns.shape[1]
    hold = alloc.shape[1]
    groups = lax.axis_size("scheme")
    parts = lax.axis_size("scen")
    cap = max(2, (2 * rows + groups - 1) // groups)
    pad = -(-cap // 16) * 16
    f32, bf16, i32 = jnp.float32, jnp.bfloat16, jnp.int32
    dma = pltpu.SemaphoreType.DMA
    book, coef, base = pl.pallas_call(
        functools.partial(kernel, groups, pad, parts),
        out_shape=(jax.ShapeDtypeStruct((1, years, n), f32),
                   jax.ShapeDtypeStruct((years, n), f32),
                   jax.ShapeDtypeStruct((1, rows), f32)),
        in_specs=[pl.BlockSpec(memory_space=pl.ANY)] * 10,
        out_specs=(pl.BlockSpec(memory_space=pltpu.VMEM),) * 3,
        scratch_shapes=[
            pltpu.VMEM((1, rows), i32),
            pltpu.VMEM((width, rows), bf16),
            pltpu.VMEM((rows, years, n), i32),
            pltpu.VMEM((hor, years, n), f32),
            pltpu.VMEM((hor, years, n), f32),
            pltpu.VMEM((years, classes, n), f32),
            pltpu.VMEM((hold, rows), i32),
            pltpu.VMEM((hold, rows), f32),
            pltpu.VMEM((1, rows), f32),
            pltpu.VMEM((1, width, n), bf16),
            pltpu.VMEM((groups * pad, width), bf16),
            pltpu.VMEM((groups * pad, width), bf16),
            pltpu.VMEM((groups * pad, years * n), bf16),
            pltpu.VMEM((groups * pad, years * n), bf16),
            pltpu.VMEM((years, width, n), f32),
            pltpu.VMEM((groups, years, n), f32),
            pltpu.VMEM((groups, years, n), f32),
            pltpu.VMEM((8, rows), f32),
            pltpu.VMEM((parts, 8, rows), f32),
            pltpu.VMEM((years + 1, n), f32),
            pltpu.VMEM((groups, years + 1, n), f32),
            dma((10,)),
            dma((groups,)), dma((groups,)),
            dma((groups,)), dma((groups,)),
            dma((groups,)), dma((groups,)),
            dma((parts,)), dma((parts,)),
            dma((groups,)), dma((groups,)),
        ],
        compiler_params=pltpu.CompilerParams(
            collective_id=0, has_side_effects=True, vmem_limit_bytes=48 * 2**20),
        name="fund",
    )(owner.T, cashflow.T, flags, rates.transpose(1, 0, 2), inflation.transpose(1, 0, 2), returns,
      alloc.T, share.T, assets0.reshape(1, rows), basis)
    levy = coef[None] * base.reshape(rows, 1, 1)
    return book, levy


def solution(mesh):
    placed = (
        P("scheme", None),
        P("scheme"),
        P("scheme", None),
        P("scheme", None),
        P("scheme", None),
        P("scheme", None, "scen"),
        P(None, None, "scen"),
        P(None, None, "scen"),
        P(None, None, "scen"),
        P("scheme", None, "scen"),
    )
    return jax.shard_map(
        shards,
        mesh=mesh,
        in_specs=placed,
        out_specs=(P("scheme", None, "scen"), P("scheme", None, "scen")),
        check_vma=False,
    )
```

time: 101 us -> 34.4 us (0.34)
  blocking collectives: 59.2 us -> 0 us
  Pallas kernels: 0 us -> 25.7 us
  starting transfers between devices: 11.1 us -> 0 us
  waiting for transfers between devices: 10 us -> 0 us
  local copies, waits for them, and re-layouts: 13.5 us -> 6.77 us
  matrix products: 2.72 us -> 0 us
  other arithmetic: 2.17 us -> 0.91 us
    unnamed x1 -> x0, blocking collectives: 35.2 us -> none
    pallas_call x0 -> x1, Pallas kernels: none -> 25.7 us  [shards(): pl.pallas_call(functools.partial(kernel, groups, pad, parts), out_shape=(...]
    psum x2 -> x0, blocking collectives: 24 us -> none  [the longest x1 17.7 us: shards(): claims, base_total = lax.psum((claim_input, jnp.sum(base)), 'scheme')]
    all_to_all x2 -> x0, starting transfers between devices: 11.1 us -> none  [the longest x1 7.41 us: shards(): lax.all_to_all(send_rows, 'scheme', split_axis=0, concat_axis=0, tiled=True)]
    all_to_all x2 -> x0, waiting for transfers between devices: 10 us -> none  [the longest x1 5.8 us: shards(): lax.all_to_all(send_rows, 'scheme', split_axis=0, concat_axis=0, tiled=True)]
    dot_general x7 -> x0, matrix products: 2.72 us -> none  [the longest x2 0.9 us: shards(): liab = jnp.dot(cashflow, disc, preferred_element_type=jnp.float32)]
    reshape x3 -> x0, local copies, waits for them, and re-layouts: 2.14 us -> none  [the longest x1 1.21 us: shards(): jnp.stack(values, axis=1).reshape(groups, count, years * scen_local)]
    scatter x1 -> x0, local copies, waits for them, and re-layouts: 1.73 us -> none  [shards(): jnp.zeros((groups * slot_cap, width), jnp.bfloat16).at[slot_pos].set(comp)]
  transfers between devices with their start and end apart: 2 -> 0, of which waited for: 2 -> 0; matrix products, arithmetic and copies ran while one was open for 5% -> 0% of each run, Pallas kernels for 0% -> 0%
where the time goes in v1:
time: 34.4 us; the launch traced here: 34.1 us
  Pallas kernels  25.7 us (75%)
  local copies, waits for them, and re-layouts  6.77 us (20%)
  other arithmetic  0.91 us (3%)
  between operations  0.68 us (2%)
    pallas_call x1, Pallas kernels, shards(): pl.pallas_call(functools.partial(kernel, groups, pad, parts), out_shape=(...  25.7 us
    unnamed x21, local copies, waits for them, and re-layouts  6.77 us
    mul x1, other arithmetic, shards(): levy = coef[None] * base.reshape(rows, 1, 1)  0.91 us

profile of v1, /device:TPU:0, one launch (start us, length us, event | category | flops | bytes accessed | tf_op | source)
XLA Modules:
  0.0 34.1 jit_solution(9980597684488512050)
XLA Ops:
  0.6 0.0 copy-start.7
  0.6 0.0 copy-start.6
  0.7 0.0 copy-start.8
  0.7 0.0 copy-start.9
  0.7 0.6 %copy-done.7 = f32[128,3]{0,1:T(4,128)S(1)} copy-done((f32[128,3]{0,1:T(4,128)S(1)}, f32[128,3]{0,1:T(4,128)}, u32[]{:S(2)}) %copy-start.7) | copy-done | bytes 1560
  1.3 0.0 copy-done.6
  1.3 0.0 copy-done.8
  1.3 0.0 copy-done.9
  1.3 0.0 copy-start
  1.3 0.9 %copy-done = s32[128,2,256]{2,1,0:T(2,128)S(1)} copy-done((s32[128,2,256]{2,1,0:T(2,128)S(1)}, s32[128,2,256]{2,1,0:T(2,128)}, u32[]{:S(2)}) %copy-start) | copy-done | bytes 262168
  2.3 0.0 copy-start.1
  2.3 0.9 %copy-done.1 = f32[2,100,256]{2,0,1:T(2,128)S(1)} copy-done((f32[2,100,256]{2,0,1:T(2,128)S(1)}, f32[2,100,256]{2,0,1:T(2,128)}, u32[]{:S(2)}) %copy-start.1) | copy-done | bytes 204824
  3.2 0.0 copy-start.2
  3.2 0.9 %copy-done.2 = f32[2,100,256]{2,0,1:T(2,128)S(1)} copy-done((f32[2,100,256]{2,0,1:T(2,128)S(1)}, f32[2,100,256]{2,0,1:T(2,128)}, u32[]{:S(2)}) %copy-start.2) | copy-done | bytes 204824
  4.2 0.0 copy-start.3
  4.2 0.9 %copy-done.3 = bf16[1,400,256]{2,1,0:T(8,128)(2,1)S(1)} copy-done((bf16[1,400,256]{2,1,0:T(8,128)(2,1)S(1)}, bf16[1,400,256]{2,1,0:T(8,128)(2,1)}, u32[]{:S(2)}) %copy-start.3) | copy-done | bytes 204824
  5.1 0.0 copy-start.4
  5.1 0.9 %copy-done.4 = bf16[128,400]{0,1:T(8,128)(2,1)S(1)} copy-done((bf16[128,400]{0,1:T(8,128)(2,1)S(1)}, bf16[128,400]{0,1:T(8,128)(2,1)}, u32[]{:S(2)}) %copy-start.4) | copy-done | bytes 102424
  6.0 0.0 copy-start.5
  6.0 0.9 %copy-done.5 = f32[2,40,256]{2,1,0:T(8,128)S(1)} copy-done((f32[2,40,256]{2,1,0:T(8,128)S(1)}, f32[2,40,256]{2,1,0:T(8,128)}, u32[]{:S(2)}) %copy-start.5) | copy-done | bytes 81944
  6.9 25.7 %fund.1 = (f32[1,2,256]{2,1,0:T(2,128)S(1)}, f32[2,256]{1,0:T(2,128)S(1)}, f32[1,128]{1,0:T(1,128)S(1)}) custom-call(s32[1,128]{1,0:T(1,128)S(1)} %bitcast.13, bf16[400,128]{1,0:T(8,128)(2,1)S(1)} %bitcast.10, s32[128,2,256]{2,1,0:T(2,128)S(1)} %copy-done, f32[100,2,256]{2,1,0:T(2,128)S(1)} %bitcast.8, f32[100,2,256]{2,1,0:T(2,128)S(1)} %bitcast.9, ...), custom_call_target="tpu_custom_call" | custom-call | tf_op jit(solution)/shard_map/fund/pallas_call | solution.py:208
  32.6 0.9 %broadcast_multiply_fusion = f32[128,2,256]{2,1,0:T(2,128)} fusion(f32[2,256]{1,0:T(2,128)S(1)} %get-tuple-element.6, f32[128]{0:T(128)S(1)} %bitcast.15), kind=kLoop, calls=%fused_computation | loop fusion | flops 65536 | bytes 264704 | tf_op jit(solution)/shard_map/mul | solution.py:249
  33.5 0.6 %copy.13 = f32[1,2,256]{2,1,0:T(2,128)} copy(f32[1,2,256]{2,1,0:T(2,128)S(1)} %get-tuple-element.10) | data formatting | bytes 4096
Async XLA Ops:
  0.6 0.7 %copy-start.7 = (f32[128,3]{0,1:T(4,128)S(1)}, f32[128,3]{0,1:T(4,128)}, u32[]{:S(2)}) copy-start(f32[128,3]{0,1:T(4,128)} %param.13) | copy-start | bytes 4612
  0.6 0.7 %copy-start.6 = (s32[128,3]{0,1:T(4,128)S(1)}, s32[128,3]{0,1:T(4,128)}, u32[]{:S(2)}) copy-start(s32[128,3]{0,1:T(4,128)} %param.12) | copy-start | bytes 4612
  0.7 0.7 %copy-start.8 = (s32[128,1]{0,1:T(1,128)S(1)}, s32[128,1]{0,1:T(1,128)}, u32[]{:S(2)}) copy-start(s32[128,1]{0,1:T(1,128)} %param.14) | copy-start | bytes 1540
  0.7 0.7 %copy-start.9 = (f32[128]{0:T(128)S(1)}, f32[128]{0:T(128)}, u32[]{:S(2)}) copy-start(f32[128]{0:T(128)} %param.11) | copy-start | bytes 1540
  1.3 1.0 %copy-start = (s32[128,2,256]{2,1,0:T(2,128)S(1)}, s32[128,2,256]{2,1,0:T(2,128)}, u32[]{:S(2)}) copy-start(s32[128,2,256]{2,1,0:T(2,128)} %flags_h.1) | copy-start | bytes 786436
  2.3 0.9 %copy-start.1 = (f32[2,100,256]{2,0,1:T(2,128)S(1)}, f32[2,100,256]{2,0,1:T(2,128)}, u32[]{:S(2)}) copy-start(f32[2,100,256]{2,0,1:T(2,128)} %param.16) | copy-start | bytes 614404
  3.2 0.9 %copy-start.2 = (f32[2,100,256]{2,0,1:T(2,128)S(1)}, f32[2,100,256]{2,0,1:T(2,128)}, u32[]{:S(2)}) copy-start(f32[2,100,256]{2,0,1:T(2,128)} %param.17) | copy-start | bytes 614404
  4.2 0.9 %copy-start.3 = (bf16[1,400,256]{2,1,0:T(8,128)(2,1)S(1)}, bf16[1,400,256]{2,1,0:T(8,128)(2,1)}, u32[]{:S(2)}) copy-start(bf16[1,400,256]{2,1,0:T(8,128)(2,1)} %basis_h.1) | copy-start | bytes 614404
  5.1 0.9 %copy-start.4 = (bf16[128,400]{0,1:T(8,128)(2,1)S(1)}, bf16[128,400]{0,1:T(8,128)(2,1)}, u32[]{:S(2)}) copy-start(bf16[128,400]{0,1:T(8,128)(2,1)} %param.10) | copy-start | bytes 307204
  6.0 0.9 %copy-start.5 = (f32[2,40,256]{2,1,0:T(8,128)S(1)}, f32[2,40,256]{2,1,0:T(8,128)}, u32[]{:S(2)}) copy-start(f32[2,40,256]{2,1,0:T(8,128)} %returns_h.1) | copy-start | bytes 245764

commit v2 on v1

--- a/solution.py
+++ b/solution.py
@@ -33,6 +33,7 @@
            owner_v, cash_v, flags_v, rates_v, infl_v, returns_v, alloc_v, share_v, assets0_v, basis_v,
            comp_send, comp_recv, flag_send, flag_recv, disc_v, held_send, held_recv,
            base_send, base_recv, claim_send, claim_recv,
+           value_v, strip_ss, strip_rs,
            local_sem, comp_ss, comp_rs, flag_ss, flag_rs, held_ss, held_rs, base_ss, base_rs, claim_ss, claim_rs):
     g = lax.axis_index("scheme")
     c = lax.axis_index("scen")
@@ -41,6 +42,9 @@
     hor = rates_v.shape[0]
     n = rates_v.shape[2]
     classes = returns_v.shape[1]
+    width = cash_v.shape[0]
+    lanes = comp_send.shape[1] // parts
+    mine = block(c, lanes)
 
     def local(k, src, dst):
         copy = pltpu.make_async_copy(src, dst, local_sem.at[k])
@@ -75,7 +79,20 @@
             device_id={"scheme": lax.rem(g + i, groups)})
 
     def comp_copy(i):
-        return to_scheme(comp_send.at[block(i, pad)], comp_recv.at[block(i, pad)], comp_ss, comp_rs, i)
+        return to_scheme(comp_send.at[block(i, pad), mine], comp_recv.at[block(i, pad), mine], comp_ss, comp_rs, i)
+
+    def strip_copy(i):
+        return pltpu.make_async_remote_copy(
+            src_ref=comp_recv.at[pad:, mine], dst_ref=comp_recv.at[pad:, mine],
+            send_sem=strip_ss.at[i], recv_sem=strip_rs.at[i],
+            device_id={"scen": lax.rem(c + i, parts)})
+
+    def strip_arrival(i):
+        strip = comp_recv.at[pad:, block(lax.rem(c - i + parts, parts), lanes)]
+        return pltpu.make_async_remote_copy(
+            src_ref=strip, dst_ref=strip,
+            send_sem=strip_ss.at[i], recv_sem=strip_rs.at[i],
+            device_id={"scen": lax.rem(c + i, parts)})
 
     def flag_copy(i):
         return to_scheme(flag_send.at[block(i, pad)], flag_recv.at[block(i, pad)], flag_ss, flag_rs, i)
@@ -101,22 +118,24 @@
     slot = rel * pad + rank
     pick = (slot == lax.broadcasted_iota(jnp.int32, (groups * pad, rows), 0)).astype(jnp.bfloat16)
 
-    in_flags.wait()
-    flags = [flags_v[:, y, :].astype(jnp.float32) for y in range(years)]
-    for y in range(years):
-        flag_send[:, y * n:(y + 1) * n] = jnp.dot(
-            pick, flags[y].astype(jnp.bfloat16), preferred_element_type=jnp.float32).astype(jnp.bfloat16)
     in_cash.wait()
     cash_t = cash_v[...]
     comp_t = jnp.minimum(0.9 * cash_t.astype(jnp.float32), COMP_LIMIT).astype(jnp.bfloat16)
-    comp_send[...] = lax.dot_general(
-        pick, comp_t, NT, preferred_element_type=jnp.float32).astype(jnp.bfloat16)
+    comp_rows = lax.dot_general(pick, comp_t, NT, preferred_element_type=jnp.float32).astype(jnp.bfloat16)
+    comp_send[:, :width] = comp_rows
+    if comp_send.shape[1] > width:
+        comp_send[:, width:] = jnp.zeros((comp_send.shape[0], comp_send.shape[1] - width), jnp.bfloat16)
 
     pl.semaphore_wait(barrier, groups + parts - 2)
     each(1, groups, lambda i: comp_copy(i).start())
+    comp_recv[0:pad, :width] = comp_rows[0:pad]
+
+    in_flags.wait()
+    flags = [flags_v[:, y, :].astype(jnp.float32) for y in range(years)]
+    for y in range(years):
+        flag_send[:, y * n:(y + 1) * n] = jnp.dot(
+            pick, flags[y].astype(jnp.bfloat16), preferred_element_type=jnp.float32).astype(jnp.bfloat16)
     each(1, groups, lambda i: flag_copy(i).start())
-    comp_recv[0:pad] = comp_send[0:pad]
-    flag_recv[0:pad] = flag_send[0:pad]
 
     in_returns.wait()
     in_alloc.wait()
@@ -139,6 +158,9 @@
                                      preferred_element_type=jnp.float32)
     each(1, groups, lambda i: held_copy(i).start())
 
+    each(1, groups, lambda i: comp_copy(i).wait_recv())
+    each(1, parts, lambda i: strip_copy(i).start())
+
     in_rates.wait()
     in_infl.wait()
     neg_terms = -(lax.broadcasted_iota(jnp.int32, (hor, n), 0) + 1).astype(jnp.float32)
@@ -159,13 +181,20 @@
     basis = basis_v[0].astype(jnp.float32)
     factors = [(basis * disc_v[y].astype(jnp.bfloat16).astype(jnp.float32)).astype(jnp.bfloat16)
                for y in range(years)]
-    each(1, groups, lambda i: comp_copy(i).wait_recv())
-    each(1, groups, lambda i: flag_copy(i).wait_recv())
-    book = []
-    for y in range(years):
-        value = jnp.dot(comp_recv[...], factors[y], preferred_element_type=jnp.float32)
-        weight = flag_recv[:, y * n:(y + 1) * n].astype(jnp.float32)
-        book.append(jnp.sum(weight * value, axis=0, keepdims=True))
+    each(1, parts, lambda i: strip_arrival(i).wait_recv())
+    for y in range(years):
+        value_v[:, y * n:(y + 1) * n] = jnp.dot(comp_recv[:, :width], factors[y],
+                                                preferred_element_type=jnp.float32)
+    value_v[0:pad] = flag_send[0:pad].astype(jnp.float32) * value_v[0:pad]
+
+    def add_book(i):
+        flag_copy(i).wait_recv()
+        at = block(i, pad)
+        value_v[0:pad] = value_v[0:pad] + flag_recv[at].astype(jnp.float32) * value_v[at]
+
+    each(1, groups, add_book)
+    summed = jnp.sum(value_v[0:pad], axis=0, keepdims=True)
+    book = [summed[:, y * n:(y + 1) * n] for y in range(years)]
     each(1, groups, lambda i: held_copy(i).wait_recv())
     held_recv[0] = held_send[0]
     for y in range(years):
@@ -188,6 +217,7 @@
         coef_ref[y:y + 1, :] = (total[y:y + 1, :] / groups) / (total[years:years + 1, :] / (rows * groups))
 
     each(1, groups, lambda i: comp_copy(i).wait_send())
+    each(1, parts, lambda i: strip_copy(i).wait_send())
     each(1, groups, lambda i: flag_copy(i).wait_send())
     each(1, groups, lambda i: held_copy(i).wait_send())
     each(1, parts, lambda i: base_copy(i).wait_send())
@@ -203,6 +233,7 @@
     parts = lax.axis_size("scen")
     cap = max(2, (2 * rows + groups - 1) // groups)
     pad = -(-cap // 16) * 16
+    lanes = -(-width // (128 * parts)) * 128
     f32, bf16, i32 = jnp.float32, jnp.bfloat16, jnp.int32
     dma = pltpu.SemaphoreType.DMA
     book, coef, base = pl.pallas_call(
@@ -210,7 +241,7 @@
         out_shape=(jax.ShapeDtypeStruct((1, years, n), f32),
                    jax.ShapeDtypeStruct((years, n), f32),
                    jax.ShapeDtypeStruct((1, rows), f32)),
-        in_specs=[pl.BlockSpec(memory_space=pl.ANY)] * 10,
+        in_specs=[pl.BlockSpec(memory_space=pltpu.HBM)] * 10,
         out_specs=(pl.BlockSpec(memory_space=pltpu.VMEM),) * 3,
         scratch_shapes=[
             pltpu.VMEM((1, rows), i32),
@@ -223,8 +254,8 @@
             pltpu.VMEM((hold, rows), f32),
             pltpu.VMEM((1, rows), f32),
             pltpu.VMEM((1, width, n), bf16),
-            pltpu.VMEM((groups * pad, width), bf16),
-            pltpu.VMEM((groups * pad, width), bf16),
+            pltpu.VMEM((groups * pad, parts * lanes), bf16),
+            pltpu.VMEM((groups * pad, parts * lanes), bf16),
             pltpu.VMEM((groups * pad, years * n), bf16),
             pltpu.VMEM((groups * pad, years * n), bf16),
             pltpu.VMEM((years, width, n), f32),
@@ -234,6 +265,8 @@
             pltpu.VMEM((parts, 8, rows), f32),
             pltpu.VMEM((years + 1, n), f32),
             pltpu.VMEM((groups, years + 1, n), f32),
+            pltpu.VMEM((groups * pad, years * n), f32),
+            dma((parts,)), dma((parts,)),
             dma((10,)),
             dma((groups,)), dma((groups,)),
             dma((groups,)), dma((groups,)),
@@ -242,7 +275,7 @@
             dma((groups,)), dma((groups,)),
         ],
         compiler_params=pltpu.CompilerParams(
-            collective_id=0, has_side_effects=True, vmem_limit_bytes=48 * 2**20),
+            collective_id=0, has_side_effects=True, vmem_limit_bytes=60 * 2**20),
         name="fund",
     )(owner.T, cashflow.T, flags, rates.transpose(1, 0, 2), inflation.transpose(1, 0, 2), returns,
       alloc.T, share.T, assets0.reshape(1, rows), basis)

time: 34.4 us -> 24 us (0.70)
  local copies, waits for them, and re-layouts: 6.77 us -> 1.23 us
  Pallas kernels: 25.7 us -> 21 us
    unnamed x21 -> x7, local copies, waits for them, and re-layouts: 6.77 us -> 1.23 us
    pallas_call x1, Pallas kernels: 25.7 us -> 21 us  [shards(): pl.pallas_call(functools.partial(kernel, groups, pad, parts), out_shape=(...]
where the time goes in v2:
time: 24 us; the launch traced here: 23.8 us
  Pallas kernels  21 us (88%)
  local copies, waits for them, and re-layouts  1.23 us (5%)
  other arithmetic  0.9 us (4%)
  between operations  0.66 us (3%)
    pallas_call x1, Pallas kernels, shards(): pl.pallas_call(functools.partial(kernel, groups, pad, parts), out_shape=(...  21 us
    unnamed x7, local copies, waits for them, and re-layouts  1.23 us
    mul x1, other arithmetic, shards(): levy = coef[None] * base.reshape(rows, 1, 1)  0.9 us

profile of v2, /device:TPU:0, one launch (start us, length us, event | category | flops | bytes accessed | tf_op | source)
XLA Modules:
  0.0 23.8 jit_solution(16567152242432514522)
XLA Ops:
  0.6 21.0 %fund.1 = (f32[1,2,256]{2,1,0:T(2,128)}, f32[2,256]{1,0:T(2,128)}, f32[1,128]{1,0:T(1,128)}) custom-call(s32[1,128]{1,0:T(1,128)} %bitcast.13, bf16[400,128]{1,0:T(8,128)(2,1)} %bitcast.10, s32[128,2,256]{2,1,0:T(2,128)} %flags_h.1, f32[100,2,256]{2,1,0:T(2,128)} %bitcast.8, f32[100,2,256]{2,1,0:T(2,128)} %bitcast.9, f32[2,40,256]{2,1,0:T(8,128)} %returns_h.1, ...), custom_call_target="tpu_custom_call" | custom-call | tf_op jit(solution)/shard_map/fund/pallas_call | solution.py:239
  21.7 0.0 copy-start
  21.7 0.0 copy-start.2
  21.7 0.6 %copy-done = f32[2,256]{1,0:T(2,128)S(1)} copy-done((f32[2,256]{1,0:T(2,128)S(1)}, f32[2,256]{1,0:T(2,128)}, u32[]{:S(2)}) %copy-start) | copy-done | bytes 2072
  22.4 0.0 copy-done.2
  22.4 0.0 copy-start.1
  22.4 0.9 %broadcast_multiply_fusion = f32[128,2,256]{2,1,0:T(2,128)} fusion(f32[2,256]{1,0:T(2,128)S(1)} %copy-done, f32[128]{0:T(128)S(1)} %bitcast.15), kind=kLoop, calls=%fused_computation | loop fusion | flops 65536 | bytes 264704 | tf_op jit(solution)/shard_map/mul | solution.py:282
  23.3 0.0 copy-done.1
  23.3 0.6 %copy.13 = f32[1,2,256]{2,1,0:T(2,128)} copy(f32[1,2,256]{2,1,0:T(2,128)S(1)} %copy-done.1) | data formatting | bytes 4096
Async XLA Ops:
  21.7 0.7 %copy-start = (f32[2,256]{1,0:T(2,128)S(1)}, f32[2,256]{1,0:T(2,128)}, u32[]{:S(2)}) copy-start(f32[2,256]{1,0:T(2,128)} %get-tuple-element.6) | copy-start | bytes 6148
  21.7 0.7 %copy-start.2 = (f32[1,128]{1,0:T(1,128)S(1)}, f32[1,128]{1,0:T(1,128)}, u32[]{:S(2)}) copy-start(f32[1,128]{1,0:T(1,128)} %get-tuple-element.7) | copy-start | bytes 1540
  22.4 0.9 %copy-start.1 = (f32[1,2,256]{2,1,0:T(2,128)S(1)}, f32[1,2,256]{2,1,0:T(2,128)}, u32[]{:S(2)}) copy-start(f32[1,2,256]{2,1,0:T(2,128)} %get-tuple-element.10) | copy-start | bytes 6148

commit v3 on v2

--- a/solution.py
+++ b/solution.py
@@ -20,6 +20,14 @@
             body(i)
     else:
         lax.fori_loop(low, high, lambda i, c: (body(i), c)[1], 0)
+
+
+def pieces(x):
+    high = x.astype(jnp.bfloat16)
+    rest = x - high.astype(jnp.float32)
+    middle = rest.astype(jnp.bfloat16)
+    low = (rest - middle.astype(jnp.float32)).astype(jnp.bfloat16)
+    return high, middle, low
 
 
 def block(i, size):
@@ -52,8 +60,8 @@
         return copy
 
     in_owner = local(0, owner_h, owner_v)
+    in_cash = local(2, cash_h, cash_v)
     in_flags = local(1, flags_h, flags_v)
-    in_cash = local(2, cash_h, cash_v)
     in_rates = local(3, rates_h, rates_v)
     in_infl = local(4, infl_h, infl_v)
     in_returns = local(5, returns_h, returns_v)
@@ -113,7 +121,8 @@
     hits = (rel == lax.broadcasted_iota(jnp.int32, (groups, rows), 0)).astype(jnp.float32)
     upper = (lax.broadcasted_iota(jnp.int32, (rows, rows), 0)
              < lax.broadcasted_iota(jnp.int32, (rows, rows), 1)).astype(jnp.bfloat16)
-    earlier = jnp.dot(hits.astype(jnp.bfloat16), upper, preferred_element_type=jnp.float32)
+    hits_b = hits.astype(jnp.bfloat16)
+    earlier = jnp.dot(hits_b, upper, preferred_element_type=jnp.float32)
     rank = jnp.sum(earlier * hits, axis=0, keepdims=True).astype(jnp.int32)
     slot = rel * pad + rank
     pick = (slot == lax.broadcasted_iota(jnp.int32, (groups * pad, rows), 0)).astype(jnp.bfloat16)
@@ -154,12 +163,10 @@
                                  preferred_element_type=jnp.float32)
         assets = assets * jnp.exp(growth)
         held.append(assets)
-        held_send[:, y, :] = jnp.dot(hits, flags[y] * assets, precision=HIGHEST,
-                                     preferred_element_type=jnp.float32)
+        held_send[:, y, :] = sum(jnp.dot(hits_b, piece, preferred_element_type=jnp.float32)
+                                 for piece in pieces(flags[y] * assets))
     each(1, groups, lambda i: held_copy(i).start())
 
-    each(1, groups, lambda i: comp_copy(i).wait_recv())
-    each(1, parts, lambda i: strip_copy(i).start())
 
     in_rates.wait()
     in_infl.wait()
@@ -173,8 +180,9 @@
         liab = lax.dot_general(cash_t, disc_v[y].astype(jnp.bfloat16), TN,
                                preferred_element_type=jnp.float32)
         short = short + (jnp.maximum(liab - held[y], 0.0) + 0.05 * liab)
-    base_send[...] = lax.dot_general(jnp.ones((8, n), jnp.float32), short, NT, precision=HIGHEST,
-                                     preferred_element_type=jnp.float32)
+    each(1, groups, lambda i: comp_copy(i).wait_recv())
+    each(1, parts, lambda i: strip_copy(i).start())
+    base_send[...] = jnp.sum(jnp.where(eye, jnp.sum(short, axis=1, keepdims=True), 0.0), axis=0, keepdims=True)
     each(1, parts, lambda i: base_copy(i).start())
 
     in_basis.wait()
@@ -203,9 +211,9 @@
         book_ref[0, y:y + 1, :] = book[y]
 
     each(1, parts, lambda i: base_copy(i).wait_recv())
-    base = base_send[0:1, :]
+    base = base_send[...]
     for i in range(1, parts):
-        base = base + base_recv[i, 0:1, :]
+        base = base + base_recv[i]
     base = base / (n * parts * years)
     base_ref[...] = base
     claim_send[years:years + 1, :] = jnp.broadcast_to(jnp.sum(base, axis=1, keepdims=True), (1, n))
@@ -222,6 +230,16 @@
     each(1, groups, lambda i: held_copy(i).wait_send())
     each(1, parts, lambda i: base_copy(i).wait_send())
     each(1, groups, lambda i: claim_copy(i).wait_send())
+
+
+def spread(book_in, coef_ref, base_ref, book_ref, levy_ref):
+    rows, years, n = levy_ref.shape
+    eye = (lax.broadcasted_iota(jnp.int32, (rows, rows), 0)
+           == lax.broadcasted_iota(jnp.int32, (rows, rows), 1))
+    base = jnp.sum(jnp.where(eye, base_ref[...], 0.0), axis=1, keepdims=True)
+    book_ref[...] = book_in[...]
+    for y in range(years):
+        levy_ref[:, y, :] = coef_ref[y:y + 1, :] * base
 
 
 def shards(cashflow, assets0, alloc, share, owner, flags, rates, inflation, returns, basis):
@@ -261,8 +279,8 @@
             pltpu.VMEM((years, width, n), f32),
             pltpu.VMEM((groups, years, n), f32),
             pltpu.VMEM((groups, years, n), f32),
-            pltpu.VMEM((8, rows), f32),
-            pltpu.VMEM((parts, 8, rows), f32),
+            pltpu.VMEM((1, rows), f32),
+            pltpu.VMEM((parts, 1, rows), f32),
             pltpu.VMEM((years + 1, n), f32),
             pltpu.VMEM((groups, years + 1, n), f32),
             pltpu.VMEM((groups * pad, years * n), f32),
@@ -275,11 +293,19 @@
             dma((groups,)), dma((groups,)),
         ],
         compiler_params=pltpu.CompilerParams(
-            collective_id=0, has_side_effects=True, vmem_limit_bytes=60 * 2**20),
+            collective_id=0, has_side_effects=True, vmem_limit_bytes=40 * 2**20),
         name="fund",
-    )(owner.T, cashflow.T, flags, rates.transpose(1, 0, 2), inflation.transpose(1, 0, 2), returns,
-      alloc.T, share.T, assets0.reshape(1, rows), basis)
-    levy = coef[None] * base.reshape(rows, 1, 1)
+    )(*(pltpu.with_memory_space_constraint(x, pltpu.HBM) for x in (
+        owner.T, cashflow.T, flags, rates.transpose(1, 0, 2), inflation.transpose(1, 0, 2), returns,
+        alloc.T, share.T, assets0.reshape(1, rows), basis)))
+    book, levy = pl.pallas_call(
+        spread,
+        out_shape=(jax.ShapeDtypeStruct((1, years, n), f32), jax.ShapeDtypeStruct((rows, years, n), f32)),
+        in_specs=[pl.BlockSpec(memory_space=pltpu.VMEM)] * 3,
+        out_specs=(pl.BlockSpec(memory_space=pltpu.VMEM),) * 2,
+        compiler_params=pltpu.CompilerParams(vmem_limit_bytes=4 * 2**20),
+        name="spread",
+    )(book, coef, base)
     return book, levy
 
 

time: 24 us -> 22.1 us (0.921)
  local copies, waits for them, and re-layouts: 1.23 us -> 0 us
  other arithmetic: 0.9 us -> 0 us
  Pallas kernels: 21 us -> 21.3 us
    unnamed x7 -> x0, local copies, waits for them, and re-layouts: 1.23 us -> none
    mul x1 -> x0, other arithmetic: 0.9 us -> none  [shards(): levy = coef[None] * base.reshape(rows, 1, 1)]
    pallas_call x0 -> x1, Pallas kernels: none -> 0.87 us  [shards(): pl.pallas_call(spread, out_shape=(jax.ShapeDtypeStruct((1, years, n), f32...]
    pallas_call x1, Pallas kernels: 21 us -> 20.5 us  [shards(): pl.pallas_call(functools.partial(kernel, groups, pad, parts), out_shape=(...]
where the time goes in v3:
time: 22.1 us; the launch traced here: 22 us
  Pallas kernels  21.3 us (96%)
  between operations  0.64 us (3%)
    pallas_call x1, Pallas kernels, shards(): pl.pallas_call(functools.partial(kernel, groups, pad, parts), out_shape=(...  20.5 us
    pallas_call x1, Pallas kernels, shards(): pl.pallas_call(spread, out_shape=(jax.ShapeDtypeStruct((1, years, n), f32...  0.87 us

profile of v3, /device:TPU:0, one launch (start us, length us, event | category | flops | bytes accessed | tf_op | source)
XLA Modules:
  0.0 22.0 jit_solution(10979454130329911034)
XLA Ops:
  0.6 20.5 %fund.1 = (f32[1,2,256]{2,1,0:T(2,128)S(1)}, f32[2,256]{1,0:T(2,128)S(1)}, f32[1,128]{1,0:T(1,128)S(1)}) custom-call(s32[1,128]{1,0:T(1,128)} %bitcast.12, bf16[400,128]{1,0:T(8,128)(2,1)} %bitcast.9, s32[128,2,256]{2,1,0:T(2,128)} %flags_h.1, f32[100,2,256]{2,1,0:T(2,128)} %bitcast.7, f32[100,2,256]{2,1,0:T(2,128)} %bitcast.8, f32[2,40,256]{2,1,0:T(8,128)} %returns_h.1, ...), custom_call_target="tpu_custom_call" | custom-call | tf_op jit(solution)/shard_map/fund/pallas_call | solution.py:257
  21.1 0.9 %spread.1 = (f32[1,2,256]{2,1,0:T(2,128)}, f32[128,2,256]{2,1,0:T(2,128)}) custom-call(f32[1,2,256]{2,1,0:T(2,128)S(1)} %get-tuple-element.5.book_in, f32[2,256]{1,0:T(2,128)S(1)} %get-tuple-element.6.coef_ref, f32[1,128]{1,0:T(1,128)S(1)} %get-tuple-element.7.base_ref), custom_call_target="tpu_custom_call" | custom-call | tf_op jit(solution)/shard_map/spread/pallas_call | solution.py:301

commit v4 on v3

--- a/solution.py
+++ b/solution.py
@@ -135,15 +135,15 @@
     if comp_send.shape[1] > width:
         comp_send[:, width:] = jnp.zeros((comp_send.shape[0], comp_send.shape[1] - width), jnp.bfloat16)
 
+    comp_recv[0:pad, :width] = comp_rows[0:pad]
+
+    in_flags.wait()
+    flags = [flags_v[:, y, :].astype(jnp.float32) for y in range(years)]
+    for y in range(years):
+        flag_send[:, y * n:(y + 1) * n] = jnp.dot(
+            pick, flags[y].astype(jnp.bfloat16), preferred_element_type=jnp.float32).astype(jnp.bfloat16)
     pl.semaphore_wait(barrier, groups + parts - 2)
     each(1, groups, lambda i: comp_copy(i).start())
-    comp_recv[0:pad, :width] = comp_rows[0:pad]
-
-    in_flags.wait()
-    flags = [flags_v[:, y, :].astype(jnp.float32) for y in range(years)]
-    for y in range(years):
-        flag_send[:, y * n:(y + 1) * n] = jnp.dot(
-            pick, flags[y].astype(jnp.bfloat16), preferred_element_type=jnp.float32).astype(jnp.bfloat16)
     each(1, groups, lambda i: flag_copy(i).start())
 
     in_returns.wait()
@@ -195,21 +195,6 @@
                                                 preferred_element_type=jnp.float32)
     value_v[0:pad] = flag_send[0:pad].astype(jnp.float32) * value_v[0:pad]
 
-    def add_book(i):
-        flag_copy(i).wait_recv()
-        at = block(i, pad)
-        value_v[0:pad] = value_v[0:pad] + flag_recv[at].astype(jnp.float32) * value_v[at]
-
-    each(1, groups, add_book)
-    summed = jnp.sum(value_v[0:pad], axis=0, keepdims=True)
-    book = [summed[:, y * n:(y + 1) * n] for y in range(years)]
-    each(1, groups, lambda i: held_copy(i).wait_recv())
-    held_recv[0] = held_send[0]
-    for y in range(years):
-        book[y] = book[y] - jnp.sum(held_recv[:, y, :], axis=0, keepdims=True)
-        claim_send[y:y + 1, :] = book[y]
-        book_ref[0, y:y + 1, :] = book[y]
-
     each(1, parts, lambda i: base_copy(i).wait_recv())
     base = base_send[...]
     for i in range(1, parts):
@@ -217,18 +202,35 @@
     base = base / (n * parts * years)
     base_ref[...] = base
     claim_send[years:years + 1, :] = jnp.broadcast_to(jnp.sum(base, axis=1, keepdims=True), (1, n))
+    each(1, groups, lambda i: held_copy(i).wait_recv())
+    held_recv[0] = held_send[0]
+    held_sum = [jnp.sum(held_recv[:, y, :], axis=0, keepdims=True) for y in range(years)]
+
+    def add_book(i):
+        flag_copy(i).wait_recv()
+        at = block(i, pad)
+        value_v[0:pad] = value_v[0:pad] + flag_recv[at].astype(jnp.float32) * value_v[at]
+
+    each(1, groups, add_book)
+    summed = jnp.sum(value_v[0:pad], axis=0, keepdims=True)
+    book = [summed[:, y * n:(y + 1) * n] for y in range(years)]
+    for y in range(years):
+        book[y] = book[y] - held_sum[y]
+        claim_send[y:y + 1, :] = book[y]
+        book_ref[0, y:y + 1, :] = book[y]
+
     each(1, groups, lambda i: claim_copy(i).start())
     claim_recv[0] = claim_send[...]
-    each(1, groups, lambda i: claim_copy(i).wait_recv())
-    total = jnp.sum(claim_recv[...], axis=0)
-    for y in range(years):
-        coef_ref[y:y + 1, :] = (total[y:y + 1, :] / groups) / (total[years:years + 1, :] / (rows * groups))
-
     each(1, groups, lambda i: comp_copy(i).wait_send())
     each(1, parts, lambda i: strip_copy(i).wait_send())
     each(1, groups, lambda i: flag_copy(i).wait_send())
     each(1, groups, lambda i: held_copy(i).wait_send())
     each(1, parts, lambda i: base_copy(i).wait_send())
+    each(1, groups, lambda i: claim_copy(i).wait_recv())
+    total = jnp.sum(claim_recv[...], axis=0)
+    for y in range(years):
+        coef_ref[y:y + 1, :] = (total[y:y + 1, :] / groups) / (total[years:years + 1, :] / (rows * groups))
+
     each(1, groups, lambda i: claim_copy(i).wait_send())
 
 

time: 22.1 us -> 22 us (level)
  no operation moved by 1% of the time
where the time goes in v4:
time: 22 us; the launch traced here: 21.8 us
  Pallas kernels  21.2 us (96%)
  between operations  0.64 us (3%)
    pallas_call x1, Pallas kernels, shards(): pl.pallas_call(functools.partial(kernel, groups, pad, parts), out_shape=(...  20.3 us
    pallas_call x1, Pallas kernels, shards(): pl.pallas_call(spread, out_shape=(jax.ShapeDtypeStruct((1, years, n), f32...  0.87 us

profile of v4, /device:TPU:0, one launch (start us, length us, event | category | flops | bytes accessed | tf_op | source)
XLA Modules:
  0.0 21.8 jit_solution(16380710666315146155)
XLA Ops:
  0.6 20.3 %fund.1 = (f32[1,2,256]{2,1,0:T(2,128)S(1)}, f32[2,256]{1,0:T(2,128)S(1)}, f32[1,128]{1,0:T(1,128)S(1)}) custom-call(s32[1,128]{1,0:T(1,128)} %bitcast.12, bf16[400,128]{1,0:T(8,128)(2,1)} %bitcast.9, s32[128,2,256]{2,1,0:T(2,128)} %flags_h.1, f32[100,2,256]{2,1,0:T(2,128)} %bitcast.7, f32[100,2,256]{2,1,0:T(2,128)} %bitcast.8, f32[2,40,256]{2,1,0:T(8,128)} %returns_h.1, ...), custom_call_target="tpu_custom_call" | custom-call | tf_op jit(solution)/shard_map/fund/pallas_call | solution.py:259
  21.0 0.9 %spread.1 = (f32[1,2,256]{2,1,0:T(2,128)}, f32[128,2,256]{2,1,0:T(2,128)}) custom-call(f32[1,2,256]{2,1,0:T(2,128)S(1)} %get-tuple-element.5.book_in, f32[2,256]{1,0:T(2,128)S(1)} %get-tuple-element.6.coef_ref, f32[1,128]{1,0:T(1,128)S(1)} %get-tuple-element.7.base_ref), custom_call_target="tpu_custom_call" | custom-call | tf_op jit(solution)/shard_map/spread/pallas_call | solution.py:303

commit v5 on v4

--- a/solution.py
+++ b/solution.py
@@ -168,26 +168,31 @@
     each(1, groups, lambda i: held_copy(i).start())
 
 
+    each(1, groups, lambda i: comp_copy(i).wait_recv())
+    each(1, parts, lambda i: strip_copy(i).start())
+
     in_rates.wait()
     in_infl.wait()
     neg_terms = -(lax.broadcasted_iota(jnp.int32, (hor, n), 0) + 1).astype(jnp.float32)
     short = jnp.zeros((rows, n), jnp.float32)
+    cash = lax.dot_general(eye.astype(jnp.bfloat16), cash_t, NT,
+                           preferred_element_type=jnp.float32).astype(jnp.bfloat16)
+    discs = []
     for y in range(years):
         rate = rates_v[:, y, :]
         infl = infl_v[:, y, :]
         for k, index in enumerate(TRANCHE_INDEX):
             disc_v[y, k * hor:(k + 1) * hor, :] = jnp.exp(neg_terms * (rate - index * infl))
-        liab = lax.dot_general(cash_t, disc_v[y].astype(jnp.bfloat16), TN,
-                               preferred_element_type=jnp.float32)
+        disc = disc_v[y].astype(jnp.bfloat16)
+        liab = jnp.dot(cash, disc, preferred_element_type=jnp.float32)
+        discs.append(disc)
         short = short + (jnp.maximum(liab - held[y], 0.0) + 0.05 * liab)
-    each(1, groups, lambda i: comp_copy(i).wait_recv())
-    each(1, parts, lambda i: strip_copy(i).start())
     base_send[...] = jnp.sum(jnp.where(eye, jnp.sum(short, axis=1, keepdims=True), 0.0), axis=0, keepdims=True)
     each(1, parts, lambda i: base_copy(i).start())
 
     in_basis.wait()
     basis = basis_v[0].astype(jnp.float32)
-    factors = [(basis * disc_v[y].astype(jnp.bfloat16).astype(jnp.float32)).astype(jnp.bfloat16)
+    factors = [(basis * discs[y].astype(jnp.float32)).astype(jnp.bfloat16)
                for y in range(years)]
     each(1, parts, lambda i: strip_arrival(i).wait_recv())
     for y in range(years):

time: 22 us -> 22 us (level)
  no operation moved by 1% of the time
where the time goes in v5:
time: 22 us; the launch traced here: 21.8 us
  Pallas kernels  21.2 us (96%)
  between operations  0.64 us (3%)
    pallas_call x1, Pallas kernels, shards(): pl.pallas_call(functools.partial(kernel, groups, pad, parts), out_shape=(...  20.3 us
    pallas_call x1, Pallas kernels, shards(): pl.pallas_call(spread, out_shape=(jax.ShapeDtypeStruct((1, years, n), f32...  0.87 us

profile of v5, /device:TPU:0, one launch (start us, length us, event | category | flops | bytes accessed | tf_op | source)
XLA Modules:
  0.0 21.8 jit_solution(6251111043337034124)
XLA Ops:
  0.6 20.3 %fund.1 = (f32[1,2,256]{2,1,0:T(2,128)S(1)}, f32[2,256]{1,0:T(2,128)S(1)}, f32[1,128]{1,0:T(1,128)S(1)}) custom-call(s32[1,128]{1,0:T(1,128)} %bitcast.12, bf16[400,128]{1,0:T(8,128)(2,1)} %bitcast.9, s32[128,2,256]{2,1,0:T(2,128)} %flags_h.1, f32[100,2,256]{2,1,0:T(2,128)} %bitcast.7, f32[100,2,256]{2,1,0:T(2,128)} %bitcast.8, f32[2,40,256]{2,1,0:T(8,128)} %returns_h.1, ...), custom_call_target="tpu_custom_call" | custom-call | tf_op jit(solution)/shard_map/fund/pallas_call | solution.py:264
  20.9 0.9 %spread.1 = (f32[1,2,256]{2,1,0:T(2,128)}, f32[128,2,256]{2,1,0:T(2,128)}) custom-call(f32[1,2,256]{2,1,0:T(2,128)S(1)} %get-tuple-element.5.book_in, f32[2,256]{1,0:T(2,128)S(1)} %get-tuple-element.6.coef_ref, f32[1,128]{1,0:T(1,128)S(1)} %get-tuple-element.7.base_ref), custom_call_target="tpu_custom_call" | custom-call | tf_op jit(solution)/shard_map/spread/pallas_call | solution.py:308
